TPU v7x, 32 devices: a whole 2x2x4 slice. The times are simulated.
32 devices in a mesh: ctx: 8 (over z, y), ch: 4 (over x, core).
Axes of the slice: x: 2, y: 2, z: 4, core: 2. Of those that a mesh axis runs over, the one named last changes fastest.
Arguments:
- tokens: bfloat16 [8192, 1536], P('ctx', 'ch'), may hold values from -6 to 6
- block_first: bfloat16 [16, 512, 512], P('ctx'), may hold values from -0.25 to 0.25
- block_second: bfloat16 [512, 16, 16], P('ctx'), may hold values from -1.5 to 1.5
- gate_weight: bfloat16 [1536, 1536], P(None, 'ch'), may hold values from -0.15625 to 0.15625
- conv_taps: float32 [4, 1536], P(None, 'ch'), may hold values from -3 to 3
- cotangent: bfloat16 [8192, 1536], P('ctx', 'ch'), may hold values from -6 to 6
Outputs:
- mixed_out: bfloat16 [8192, 1536], P('ctx', 'ch')
- grad_tokens: bfloat16 [8192, 1536], P('ctx', 'ch')
- grad_taps: float32 [4, 1536], P(None, 'ch')
- grad_gate_weight: float32 [1536, 1536], P(None, 'ch')
- grad_first: float32 [16, 512, 512], P('ctx')
- grad_second: float32 [512, 16, 16], P('ctx')
All inputs are finite; a program needn't handle non-finite values.
Results may differ from a plain program's by a relative error of at most 0.0064.
Values may be sent and summed in bfloat16 or wider, within the bound.
No kernel may reach another device: no remote copies, remote signals or barrier semaphores. Data moves between devices by JAX's collectives and lax.ppermute only.
A program may use at most 64 MiB of HBM per device.

v0:
```python
import jax
import jax.numpy as jnp
from jax import lax
from jax.sharding import PartitionSpec as P


def passed_along(array, axis, by):
    count = lax.axis_size(axis)
    pairs = [(i, i + by) for i in range(count) if 0 <= i + by < count]
    return lax.ppermute(array, axis, pairs)


def on_device(tokens, block_first, block_second, gate_weight, conv_taps, cotangent):
    blocks = block_first.shape[0]
    block_size = block_first.shape[1]
    tok_rows = tokens.shape[0]
    chan_count = tokens.shape[1]
    tap_count = conv_taps.shape[0]
    local_blocks = tokens.reshape(blocks, block_size, chan_count)
    first_out = jnp.einsum(
        "nrs,nsc->nrc", block_first, local_blocks, preferred_element_type=jnp.float32
    ).astype(jnp.bfloat16)
    columns = lax.all_to_all(first_out, "ctx", split_axis=1, concat_axis=0, tiled=True)
    second_out = jnp.einsum(
        "rmn,nrc->mrc", block_second, columns, preferred_element_type=jnp.float32
    ).astype(jnp.bfloat16)
    mixed_seq = lax.all_to_all(second_out, "ctx", split_axis=0, concat_axis=1, tiled=True).reshape(
        tok_rows, chan_count
    )
    features = lax.all_gather(tokens, "ch", axis=1, tiled=True)
    gate_pre = jnp.dot(features, gate_weight, preferred_element_type=jnp.float32)
    gate_sig = jax.nn.sigmoid(gate_pre)
    mixed_wide = mixed_seq.astype(jnp.float32)
    gated_vals = (mixed_wide * gate_sig).astype(jnp.bfloat16)
    earlier = passed_along(gated_vals[tok_rows - (tap_count - 1) :], "ctx", 1)
    padded = jnp.concatenate([earlier, gated_vals], 0).astype(jnp.float32)
    conv_out = jnp.zeros((tok_rows, chan_count), jnp.float32)
    for offset in range(tap_count):
        conv_out = (
            conv_out
            + conv_taps[offset][None, :]
            * padded[tap_count - 1 - offset : tap_count - 1 - offset + tok_rows]
        )
    mixed_out = conv_out.astype(jnp.bfloat16)
    following = passed_along(cotangent[: tap_count - 1], "ctx", -1)
    cot_wide = cotangent.astype(jnp.float32)
    cot_pad = jnp.concatenate([cotangent, following], 0).astype(jnp.float32)
    grad_gated = jnp.zeros((tok_rows, chan_count), jnp.float32)
    tap_rows = []
    for offset in range(tap_count):
        grad_gated = grad_gated + conv_taps[offset][None, :] * cot_pad[offset : offset + tok_rows]
        tap_rows.append(
            jnp.sum(
                cot_wide * padded[tap_count - 1 - offset : tap_count - 1 - offset + tok_rows], 0
            )
        )
    tap_part = jnp.stack(tap_rows, 0)
    grad_mix = (grad_gated * gate_sig).astype(jnp.bfloat16)
    grad_gate = (grad_gated * mixed_wide * gate_sig * (1.0 - gate_sig)).astype(jnp.bfloat16)
    weight_part = lax.dot_general(
        features, grad_gate, (((0,), (0,)), ((), ())), preferred_element_type=jnp.float32
    )
    grad_taps, grad_gate_weight = lax.psum((tap_part, weight_part), "ctx")
    full_part = lax.dot_general(
        grad_gate, gate_weight, (((1,), (1,)), ((), ())), preferred_element_type=jnp.float32
    )
    gate_input_grad = lax.psum_scatter(
        full_part.astype(jnp.bfloat16), "ch", scatter_dimension=1, tiled=True
    ).astype(jnp.float32)
    grad_cols = lax.all_to_all(
        grad_mix.reshape(blocks, block_size, chan_count),
        "ctx",
        split_axis=1,
        concat_axis=0,
        tiled=True,
    )
    second_part = jnp.einsum("mrc,nrc->rmn", grad_cols, columns, preferred_element_type=jnp.float32)
    grad_first_t = jnp.einsum(
        "rmn,mrc->nrc", block_second, grad_cols, preferred_element_type=jnp.float32
    ).astype(jnp.bfloat16)
    grad_back = lax.all_to_all(grad_first_t, "ctx", split_axis=0, concat_axis=1, tiled=True)
    first_part = jnp.einsum(
        "nrc,nsc->nrs", grad_back, local_blocks, preferred_element_type=jnp.float32
    )
    grad_local = jnp.einsum(
        "nrs,nrc->nsc", block_first, grad_back, preferred_element_type=jnp.float32
    ).reshape(tok_rows, chan_count)
    grad_tokens = (grad_local + gate_input_grad).astype(jnp.bfloat16)
    grad_first, grad_second = lax.psum((first_part, second_part), "ch")
    return (mixed_out, grad_tokens, grad_taps, grad_gate_weight, grad_first, grad_second)


def solution(mesh):
    in_specs = (
        P("ctx", "ch"),
        P("ctx", None, None),
        P("ctx", None, None),
        P(None, "ch"),
        P(None, "ch"),
        P("ctx", "ch"),
    )
    out_specs = (
        P("ctx", "ch"),
        P("ctx", "ch"),
        P(None, "ch"),
        P(None, "ch"),
        P("ctx", None, None),
        P("ctx", None, None),
    )
    return jax.shard_map(
        on_device, mesh=mesh, in_specs=in_specs, out_specs=out_specs, check_vma=False
    )
```

profile of v0, /device:TPU:0, one launch (start us, length us, event | category | flops | bytes accessed | tf_op | source)
XLA Modules:
  0.0 322.3 jit_solution(4741320819189164294)
XLA Ops:
  7.9 2.2 convolution_convert_fusion.1
  10.1 1.7 copy.44
  11.8 7.3 %all-to-all-start = ((bf16[2,512,384]{2,0,1:T(2,128)(2,1)}), bf16[2,512,384]{2,0,1:T(2,128)(2,1)S(1)}, u32[]{:S(2)}, u32[]{:S(2)}) async-start(bf16[2,512,384]{2,0,1:T(2,128)(2,1)} %copy.44), calls=%async_computation | async-start | bytes 1572864 | tf_op jit(solution)/shard_map/all_to_all | solution.py:23
  20.1 19.2 %all-to-all-done = bf16[2,512,384]{2,0,1:T(2,128)(2,1)S(1)} async-done(((bf16[2,512,384]{2,0,1:T(2,128)(2,1)}), bf16[2,512,384]{2,0,1:T(2,128)(2,1)S(1)}, u32[]{:S(2)}, u32[]{:S(2)}) %all-to-all-start) | async-done | bytes 786464 | tf_op jit(solution)/shard_map/all_to_all | solution.py:23
  42.3 3.6 %all-to-all-start.1 = ((bf16[16,64,384]{2,1,0:T(8,128)(2,1)}), bf16[16,64,384]{2,1,0:T(8,128)(2,1)S(1)}, u32[]{:S(2)}, u32[]{:S(2)}) async-start(bf16[16,64,384]{2,1,0:T(8,128)(2,1)} %copy.47), calls=%async_computation.1 | async-start | bytes 1572864 | tf_op jit(solution)/shard_map/all_to_all | solution.py:27
  48.0 4.0 %collective-permute-done.1 = bf16[3,384]{1,0:T(4,128)(2,1)S(1)} collective-permute-done((bf16[3,384]{1,0:T(4,128)(2,1)S(1)}, bf16[3,384]{1,0:T(4,128)(2,1)S(1)}, u32[]{:S(2)}, u32[]{:S(2)}) %collective-permute-start.1) | collective-permute-done | bytes 2336 | tf_op jit(solution)/shard_map/ppermute | solution.py:10
  53.3 13.0 %all-to-all-done.1 = bf16[16,64,384]{2,1,0:T(8,128)(2,1)S(1)} async-done(((bf16[16,64,384]{2,1,0:T(8,128)(2,1)}), bf16[16,64,384]{2,1,0:T(8,128)(2,1)S(1)}, u32[]{:S(2)}, u32[]{:S(2)}) %all-to-all-start.1) | async-done | bytes 786464 | tf_op jit(solution)/shard_map/all_to_all | solution.py:27
  67.6 8.1 %fusion.10 = (bf16[1024,384]{1,0:T(8,128)(2,1)}, f32[1024,384]{1,0:T(8,128)S(1)}, bf16[1024,384]{1,0:T(8,128)(2,1)}, f32[1024,384]{1,0:T(8,128)S(1)}) fusion(f32[8,2,64,384]{3,2,0,1:T(8,128)} %copy.48, f32[1027,384]{1,0:T(8,128)} %maximum_convert_fusion.1, f32[384]{0:T(512)S(1)} %get-tuple-element.36, f32[384]{0:T(512)S(1)} %get-tuple-element.37, ...), kind=kOutput, calls=%fused_computation.22 | convolution fusion | flops 1214644224 | bytes 16914432 | tf_op jit(solution)/shard_map/dot_general | solution.py:31
  75.9 1.7 copy.49
  77.6 4.0 %all-to-all-start.2 = ((bf16[2,512,384]{2,0,1:T(2,128)(2,1)}), bf16[2,512,384]{2,0,1:T(2,128)(2,1)S(1)}, u32[]{:S(2)}, u32[]{:S(2)}) async-start(bf16[2,512,384]{2,0,1:T(2,128)(2,1)} %copy.49), calls=%async_computation.2 | async-start | bytes 1572864 | tf_op jit(solution)/shard_map/all_to_all | solution.py:70
  81.6 5.0 %convolution_bitcast_fusion = f32[1536,384]{0,1:T(8,128)} fusion(bf16[1024,384]{1,0:T(8,128)(2,1)} %get-tuple-element.40, bf16[1024,1536]{1,0:T(8,128)(2,1)} %all-gather.2.cloned.1.call-done), kind=kOutput, calls=%fused_computation.1 | convolution fusion | flops 1207959552 | bytes 6291456 | tf_op jit(solution)/shard_map/dot_general | solution.py:60
  86.6 28.1 %all-to-all-done.2 = bf16[2,512,384]{2,0,1:T(2,128)(2,1)S(1)} async-done(((bf16[2,512,384]{2,0,1:T(2,128)(2,1)}), bf16[2,512,384]{2,0,1:T(2,128)(2,1)S(1)}, u32[]{:S(2)}, u32[]{:S(2)}) %all-to-all-start.2) | async-done | bytes 786464 | tf_op jit(solution)/shard_map/all_to_all | solution.py:70
  114.7 1.4 copy.63
  116.1 2.3 all_to_all.54
  118.4 1.4 fusion.13
  120.8 4.2 %all-to-all-start.3 = ((bf16[16,64,384]{2,1,0:T(8,128)(2,1)}), bf16[16,64,384]{2,1,0:T(8,128)(2,1)}, u32[]{:S(2)}, u32[]{:S(2)}) async-start(bf16[16,64,384]{2,1,0:T(8,128)(2,1)} %copy.52), calls=%async_computation.3 | async-start | bytes 1572864 | tf_op jit(solution)/shard_map/all_to_all | solution.py:81
  126.4 20.1 %all-to-all-done.3 = bf16[16,64,384]{2,1,0:T(8,128)(2,1)} async-done(((bf16[16,64,384]{2,1,0:T(8,128)(2,1)}), bf16[16,64,384]{2,1,0:T(8,128)(2,1)}, u32[]{:S(2)}, u32[]{:S(2)}) %all-to-all-start.3) | async-done | bytes 786464 | tf_op jit(solution)/shard_map/all_to_all | solution.py:81
  147.7 2.1 fusion.15
  150.9 3.5 %convolution_convert_fusion = bf16[1024,1536]{1,0:T(8,128)(2,1)} fusion(bf16[1024,384]{1,0:T(8,128)(2,1)S(1)} %copy-done.7, bf16[1536,384]{1,0:T(8,128)(2,1)S(1)} %copy-done), kind=kOutput, calls=%fused_computation | convolution fusion | flops 1209532416 | bytes 5111808 | tf_op jit(solution)/shard_map/dot_general | solution.py:64
  154.4 4.6 %copy.59 = bf16[1024,1536]{0,1:T(8,128)(2,1)} copy(bf16[1024,1536]{1,0:T(8,128)(2,1)} %convolution_convert_fusion) | data formatting | bytes 6291456
  160.2 3.8 %collective-permute-start = (bf16[3,384]{1,0:T(4,128)(2,1)S(1)}, bf16[3,384]{1,0:T(4,128)(2,1)S(1)}, u32[]{:S(2)}, u32[]{:S(2)}) collective-permute-start(bf16[3,384]{1,0:T(4,128)(2,1)S(1)} %slice.64), channel_id=1, source_target_pairs={{0,4},{4,8},{8,12},{12,16},{16,20},{20,24},{24,28},{1,5},{5,9},{9,... | collective-permute-start | bytes 6920 | tf_op jit(solution)/shard_map/ppermute | solution.py:10
  165.6 2.1 fusion
  167.7 21.6 %psum.28 = f32[4,384]{1,0:T(4,128)} all-reduce(f32[4,384]{1,0:T(4,128)S(1)} %pad_maximum_fusion), channel_id=1, replica_groups=mesh['ctx'=8,'ch'=4] {'ctx'}, use_global_device_ids=true, to_apply=%region_5.0 | all-reduce | flops 1536 | bytes 12288 | tf_op jit(solution)/shard_map/psum | solution.py:63
  189.3 19.1 %all-reduce.4.cloned.1.call-done = f32[1536,384]{0,1:T(8,128)} async-done(((f32[1536,384]{0,1:T(8,128)}), f32[1536,384]{0,1:T(8,128)}) %all-reduce.4.cloned.1.call-update) | async-done | bytes 2359312 | tf_op jit(solution)/shard_map/psum | solution.py:63
  208.4 3.0 copy.56
  211.5 3.0 convolution_bitcast_fusion.1
  214.5 1.9 copy.55
  216.3 54.4 %all-reduce.6.cloned.1.call-done = (f32[2,512,512]{2,1,0:T(8,128)}, f32[64,16,16]{2,1,0:T(8,128)}) async-done(((f32[2,512,512]{2,1,0:T(8,128)}, f32[64,16,16]{2,1,0:T(8,128)}), (f32[2,512,512]{2,1,0:T(8,128)}, f32[64,16,16]{2,1,0:T(8,128)})) %all-reduce.6.cloned.1.call-update) | async-done | bytes 2162704 | tf_op jit(solution)/shard_map/psum | solution.py:89
  270.7 1.9 copy.57
  272.6 38.5 %reduce-scatter.4.cloned.1.call-done = bf16[384,1024]{1,0:T(8,128)(2,1)} async-done(((bf16[1536,1024]{1,0:T(8,128)(2,1)}), bf16[384,1024]{1,0:T(8,128)(2,1)}) %reduce-scatter.4.cloned.1.call-update) | async-done | bytes 786448
  311.1 1.5 copy.60
  314.5 1.3 copy.68
  (48 shorter events, 18.9 us)
Async XLA Ops:
  7.2 60.4 %copy-start = (bf16[1536,384]{1,0:T(8,128)(2,1)S(1)}, bf16[1536,384]{1,0:T(8,128)(2,1)}, u32[]{:S(2)}) copy-start(bf16[1536,384]{1,0:T(8,128)(2,1)} %param.9) | copy-start | bytes 3538948
  7.2 60.4 %all-gather.2.cloned.1.call-start = ((), (), s32[]{:S(2)}) async-start(), calls=%async_computation.5 | async-start | bytes 3932160 | tf_op jit(solution)/shard_map/all_gather | solution.py:30
  10.1 9.0 %copy-start.6 = (bf16[64,16,16]{0,2,1:T(8,128)(2,1)S(1)}, bf16[64,16,16]{0,2,1:T(8,128)(2,1)}, u32[]{:S(2)}) copy-start(bf16[64,16,16]{0,2,1:T(8,128)(2,1)} %param.8) | copy-start | bytes 98308
  11.8 27.5 %all-to-all-start = ((bf16[2,512,384]{2,0,1:T(2,128)(2,1)}), bf16[2,512,384]{2,0,1:T(2,128)(2,1)S(1)}, u32[]{:S(2)}, u32[]{:S(2)}) async-start(bf16[2,512,384]{2,0,1:T(2,128)(2,1)} %copy.44), calls=%async_computation | async-start | bytes 1572864 | tf_op jit(solution)/shard_map/all_to_all | solution.py:23
  39.8 1.0 copy-start.3
  41.2 4.6 %copy-start.1 = (bf16[1024,384]{1,0:T(8,128)(2,1)S(1)}, bf16[1024,384]{1,0:T(8,128)(2,1)}, u32[]{:S(2)}) copy-start(bf16[1024,384]{1,0:T(8,128)(2,1)} %param.11) | copy-start | bytes 2359300
  42.3 24.0 %all-to-all-start.1 = ((bf16[16,64,384]{2,1,0:T(8,128)(2,1)}), bf16[16,64,384]{2,1,0:T(8,128)(2,1)S(1)}, u32[]{:S(2)}, u32[]{:S(2)}) async-start(bf16[16,64,384]{2,1,0:T(8,128)(2,1)} %copy.47), calls=%async_computation.1 | async-start | bytes 1572864 | tf_op jit(solution)/shard_map/all_to_all | solution.py:27
  45.8 6.2 %collective-permute-start.1 = (bf16[3,384]{1,0:T(4,128)(2,1)S(1)}, bf16[3,384]{1,0:T(4,128)(2,1)S(1)}, u32[]{:S(2)}, u32[]{:S(2)}) collective-permute-start(bf16[3,384]{1,0:T(4,128)(2,1)S(1)} %slice.59), channel_id=1, source_target_pairs={{4,0},{8,4},{12,8},{16,12},{20,16},{24,20},{28,24},{5,1},{9,5},{13... | collective-permute-start | bytes 6920 | tf_op jit(solution)/shard_map/ppermute | solution.py:10
  77.6 37.1 %all-to-all-start.2 = ((bf16[2,512,384]{2,0,1:T(2,128)(2,1)}), bf16[2,512,384]{2,0,1:T(2,128)(2,1)S(1)}, u32[]{:S(2)}, u32[]{:S(2)}) async-start(bf16[2,512,384]{2,0,1:T(2,128)(2,1)} %copy.49), calls=%async_computation.2 | async-start | bytes 1572864 | tf_op jit(solution)/shard_map/all_to_all | solution.py:70
  81.6 126.8 %all-reduce.4.cloned.1.call-start = ((), (), s32[]{:S(2)}) async-start(), calls=%async_computation.6 | async-start | bytes 4718592 | tf_op jit(solution)/shard_map/psum | solution.py:63
  120.8 25.6 %all-to-all-start.3 = ((bf16[16,64,384]{2,1,0:T(8,128)(2,1)}), bf16[16,64,384]{2,1,0:T(8,128)(2,1)}, u32[]{:S(2)}, u32[]{:S(2)}) async-start(bf16[16,64,384]{2,1,0:T(8,128)(2,1)} %copy.52), calls=%async_computation.3 | async-start | bytes 1572864 | tf_op jit(solution)/shard_map/all_to_all | solution.py:81
  125.0 145.7 %all-reduce.6.cloned.1.call-start = ((), (), s32[]{:S(2)}) async-start(), calls=%async_computation.8 | async-start | bytes 5242880 | tf_op jit(solution)/shard_map/psum | solution.py:89
  126.4 21.3 %copy-start.2 = (bf16[1024,384]{1,0:T(8,128)(2,1)S(1)}, bf16[1024,384]{1,0:T(8,128)(2,1)}, u32[]{:S(2)}) copy-start(bf16[1024,384]{1,0:T(8,128)(2,1)} %param.6) | copy-start | bytes 2359300
  149.7 1.1 copy-start.7
  149.8 161.3 %reduce-scatter.4.cloned.1.call-start = ((), (), s32[]{:S(2)}) async-start(), calls=%async_computation.7 | async-start | bytes 3932160
  159.1 1.2 copy-start.5
  160.2 5.1 %collective-permute-start = (bf16[3,384]{1,0:T(4,128)(2,1)S(1)}, bf16[3,384]{1,0:T(4,128)(2,1)S(1)}, u32[]{:S(2)}, u32[]{:S(2)}) collective-permute-start(bf16[3,384]{1,0:T(4,128)(2,1)S(1)} %slice.64), channel_id=1, source_target_pairs={{0,4},{4,8},{8,12},{12,16},{16,20},{20,24},{24,28},{1,5},{5,9},{9,... | collective-permute-start | bytes 6920 | tf_op jit(solution)/shard_map/ppermute | solution.py:10
  312.6 1.9 copy-start.4
Sparse Core Ops, SparseCore 0:
  9.6 31.1 all-gather.1
  86.7 121.6 all-reduce.3
  211.5 59.1 all-reduce.5
  273.1 37.9 reduce-scatter.3
where the time goes:
time: 323 us; the launch traced here: 322 us
  waiting for transfers between devices  198 us (61%)
  local copies, waits for them, and re-layouts  32.2 us (10%)
  matrix products  26.9 us (8%)
  starting transfers between devices  24.6 us (8%)
  blocking collectives  21.6 us (7%)
  between operations  14 us (4%)
  other arithmetic  4.69 us (1%)
    psum x1, waiting for transfers between devices, on_device(): grad_first, grad_second = lax.psum((first_part, second_part), 'ch')  54.4 us
    unnamed x5, waiting for transfers between devices  39.2 us
    all_to_all x1, waiting for transfers between devices, on_device(): lax.all_to_all(grad_mix.reshape(blocks, block_size, chan_count), 'ctx', s...  28.1 us
    psum x1, blocking collectives, on_device(): grad_taps, grad_gate_weight = lax.psum((tap_part, weight_part), 'ctx')  21.6 us
    all_to_all x1, waiting for transfers between devices, on_device(): lax.all_to_all(grad_first_t, 'ctx', split_axis=0, concat_axis=1, tiled=True)  20.1 us
    all_to_all x1, waiting for transfers between devices, on_device(): lax.all_to_all(first_out, 'ctx', split_axis=1, concat_axis=0, tiled=True)  19.2 us
    psum x1, waiting for transfers between devices, on_device(): grad_taps, grad_gate_weight = lax.psum((tap_part, weight_part), 'ctx')  19.1 us
    unnamed x22, local copies, waits for them, and re-layouts  16.9 us
  transfers between devices with their start and end apart: 10, of which 9 were waited for; matrix products, arithmetic and copies ran while one was open for 14% of the time, Pallas kernels for 0%

commit v1 on v0

--- a/solution.py
+++ b/solution.py
@@ -67,12 +67,18 @@
     gate_input_grad = lax.psum_scatter(
         full_part.astype(jnp.bfloat16), "ch", scatter_dimension=1, tiled=True
     ).astype(jnp.float32)
-    grad_cols = lax.all_to_all(
-        grad_mix.reshape(blocks, block_size, chan_count),
-        "ctx",
-        split_axis=1,
-        concat_axis=0,
-        tiled=True,
+    grad_cols = jnp.concatenate(
+        lax.all_to_all(
+            jnp.stack(
+                jnp.split(
+                    grad_mix.reshape(blocks, block_size, chan_count), lax.axis_size("ctx"), axis=1
+                )
+            ),
+            "ctx",
+            0,
+            0,
+        ),
+        axis=0,
     )
     second_part = jnp.einsum("mrc,nrc->rmn", grad_cols, columns, preferred_element_type=jnp.float32)
     grad_first_t = jnp.einsum(

time: 323 us -> 331 us (1.025)
  waiting for transfers between devices: 198 us -> 207 us
    psum x1, waiting for transfers between devices: 19.1 us -> 27.3 us  [on_device(): grad_taps, grad_gate_weight = lax.psum((tap_part, weight_part), 'ctx')]
    unnamed x22 -> x29, local copies, waits for them, and re-layouts: 16.9 us -> 21.6 us
    all_to_all x2 -> x0, local copies, waits for them, and re-layouts: 3.69 us -> none  [on_device(): lax.all_to_all(grad_mix.reshape(blocks, block_size, chan_count), 'ctx', s...]
  transfers between devices with their start and end apart: 10 -> 10, of which waited for: 9 -> 9; matrix products, arithmetic and copies ran while one was open for 14% -> 13% of each run, Pallas kernels for 0% -> 0%
where the time goes in v1:
time: 331 us; the launch traced here: 330 us
  waiting for transfers between devices  207 us (63%)
  local copies, waits for them, and re-layouts  32.2 us (10%)
  matrix products  27.2 us (8%)
  starting transfers between devices  24 us (7%)
  blocking collectives  21.4 us (6%)
  between operations  14 us (4%)
  other arithmetic  4.69 us (1%)
    psum x1, waiting for transfers between devices, on_device(): grad_first, grad_second = lax.psum((first_part, second_part), 'ch')  54.3 us
    unnamed x5, waiting for transfers between devices  39.2 us
    all_to_all x1, waiting for transfers between devices, on_device(): lax.all_to_all(jnp.stack(jnp.split(grad_mix.reshape(blocks, block_size, c...  28.1 us
    psum x1, waiting for transfers between devices, on_device(): grad_taps, grad_gate_weight = lax.psum((tap_part, weight_part), 'ctx')  27.3 us
    unnamed x29, local copies, waits for them, and re-layouts  21.6 us
    psum x1, blocking collectives, on_device(): grad_taps, grad_gate_weight = lax.psum((tap_part, weight_part), 'ctx')  21.4 us
    all_to_all x1, waiting for transfers between devices, on_device(): lax.all_to_all(grad_first_t, 'ctx', split_axis=0, concat_axis=1, tiled=True)  20.8 us
    all_to_all x1, waiting for transfers between devices, on_device(): lax.all_to_all(first_out, 'ctx', split_axis=1, concat_axis=0, tiled=True)  19.2 us
  transfers between devices with their start and end apart: 10, of which 9 were waited for; matrix products, arithmetic and copies ran while one was open for 13% of the time, Pallas kernels for 0%

profile of v1, /device:TPU:0, one launch (start us, length us, event | category | flops | bytes accessed | tf_op | source)
XLA Modules:
  0.0 330.3 jit_solution(500461419207449065)
XLA Ops:
  7.9 2.2 convolution_convert_fusion.1
  10.1 1.7 copy.43
  11.8 7.3 %all-to-all-start = ((bf16[2,512,384]{2,0,1:T(2,128)(2,1)}), bf16[2,512,384]{2,0,1:T(2,128)(2,1)S(1)}, u32[]{:S(2)}, u32[]{:S(2)}) async-start(bf16[2,512,384]{2,0,1:T(2,128)(2,1)} %copy.43), calls=%async_computation | async-start | bytes 1572864 | tf_op jit(solution)/shard_map/all_to_all | solution.py:23
  20.1 19.2 %all-to-all-done = bf16[2,512,384]{2,0,1:T(2,128)(2,1)S(1)} async-done(((bf16[2,512,384]{2,0,1:T(2,128)(2,1)}), bf16[2,512,384]{2,0,1:T(2,128)(2,1)S(1)}, u32[]{:S(2)}, u32[]{:S(2)}) %all-to-all-start) | async-done | bytes 786464 | tf_op jit(solution)/shard_map/all_to_all | solution.py:23
  42.3 3.6 %all-to-all-start.1 = ((bf16[16,64,384]{2,1,0:T(8,128)(2,1)}), bf16[16,64,384]{2,1,0:T(8,128)(2,1)S(1)}, u32[]{:S(2)}, u32[]{:S(2)}) async-start(bf16[16,64,384]{2,1,0:T(8,128)(2,1)} %copy.46), calls=%async_computation.1 | async-start | bytes 1572864 | tf_op jit(solution)/shard_map/all_to_all | solution.py:27
  45.8 1.3 collective-permute-start.1
  48.0 4.0 %collective-permute-done.1 = bf16[3,384]{1,0:T(4,128)(2,1)S(1)} collective-permute-done((bf16[3,384]{1,0:T(4,128)(2,1)S(1)}, bf16[3,384]{1,0:T(4,128)(2,1)S(1)}, u32[]{:S(2)}, u32[]{:S(2)}) %collective-permute-start.1) | collective-permute-done | bytes 2336 | tf_op jit(solution)/shard_map/ppermute | solution.py:10
  53.3 13.0 %all-to-all-done.1 = bf16[16,64,384]{2,1,0:T(8,128)(2,1)S(1)} async-done(((bf16[16,64,384]{2,1,0:T(8,128)(2,1)}), bf16[16,64,384]{2,1,0:T(8,128)(2,1)S(1)}, u32[]{:S(2)}, u32[]{:S(2)}) %all-to-all-start.1) | async-done | bytes 786464 | tf_op jit(solution)/shard_map/all_to_all | solution.py:27
  66.3 1.3 copy.47
  67.6 8.1 %fusion.10 = (bf16[1024,384]{1,0:T(8,128)(2,1)}, f32[1024,384]{1,0:T(8,128)S(1)}, bf16[1024,384]{1,0:T(8,128)(2,1)}, f32[1024,384]{1,0:T(8,128)S(1)}) fusion(f32[8,2,64,384]{3,2,0,1:T(8,128)} %copy.47, f32[1027,384]{1,0:T(8,128)} %maximum_convert_fusion.1, f32[384]{0:T(512)S(1)} %get-tuple-element.36, f32[384]{0:T(512)S(1)} %get-tuple-element.37, ...), kind=kOutput, calls=%fused_computation.22 | convolution fusion | flops 1214644224 | bytes 16914432 | tf_op jit(solution)/shard_map/dot_general | solution.py:31
  81.1 4.0 %all-to-all-start.2 = ((bf16[8,2,64,384]{3,2,1,0:T(8,128)(2,1)}), bf16[8,2,64,384]{3,2,1,0:T(8,128)(2,1)S(1)}, u32[]{:S(2)}, u32[]{:S(2)}) async-start(bf16[8,2,64,384]{3,2,1,0:T(8,128)(2,1)} %fusion.17), calls=%async_computation.2 | async-start | bytes 1572864 | tf_op jit(solution)/shard_map/all_to_all | solution.py:71
  85.2 5.0 %convolution_bitcast_fusion = f32[1536,384]{0,1:T(8,128)} fusion(bf16[1024,384]{1,0:T(8,128)(2,1)} %get-tuple-element.40, bf16[1024,1536]{1,0:T(8,128)(2,1)} %all-gather.2.cloned.1.call-done), kind=kOutput, calls=%fused_computation.1 | convolution fusion | flops 1207959552 | bytes 6291456 | tf_op jit(solution)/shard_map/dot_general | solution.py:60
  90.1 28.1 %all-to-all-done.2 = bf16[8,2,64,384]{3,2,1,0:T(8,128)(2,1)S(1)} async-done(((bf16[8,2,64,384]{3,2,1,0:T(8,128)(2,1)}), bf16[8,2,64,384]{3,2,1,0:T(8,128)(2,1)S(1)}, u32[]{:S(2)}, u32[]{:S(2)}) %all-to-all-start.2) | async-done | bytes 786464 | tf_op jit(solution)/shard_map/all_to_all | solution.py:71
  118.2 1.5 fusion.13
  120.8 4.2 %all-to-all-start.3 = ((bf16[16,64,384]{2,1,0:T(8,128)(2,1)}), bf16[16,64,384]{2,1,0:T(8,128)(2,1)}, u32[]{:S(2)}, u32[]{:S(2)}) async-start(bf16[16,64,384]{2,1,0:T(8,128)(2,1)} %copy.50), calls=%async_computation.3 | async-start | bytes 1572864 | tf_op jit(solution)/shard_map/all_to_all | solution.py:87
  125.1 1.4 fusion.14
  126.5 20.8 %all-to-all-done.3 = bf16[16,64,384]{2,1,0:T(8,128)(2,1)} async-done(((bf16[16,64,384]{2,1,0:T(8,128)(2,1)}), bf16[16,64,384]{2,1,0:T(8,128)(2,1)}, u32[]{:S(2)}, u32[]{:S(2)}) %all-to-all-start.3) | async-done | bytes 786464 | tf_op jit(solution)/shard_map/all_to_all | solution.py:87
  148.5 2.1 fusion.26
  151.7 3.5 %convolution_convert_fusion = bf16[1024,1536]{1,0:T(8,128)(2,1)} fusion(bf16[1024,384]{1,0:T(8,128)(2,1)S(1)} %copy-done.7, bf16[1536,384]{1,0:T(8,128)(2,1)S(1)} %copy-done), kind=kOutput, calls=%fused_computation | convolution fusion | flops 1209532416 | bytes 5111808 | tf_op jit(solution)/shard_map/dot_general | solution.py:64
  155.2 4.7 %copy.58 = bf16[1024,1536]{0,1:T(8,128)(2,1)} copy(bf16[1024,1536]{1,0:T(8,128)(2,1)} %convolution_convert_fusion) | data formatting | bytes 6291456
  161.0 3.4 %collective-permute-start = (bf16[3,384]{1,0:T(4,128)(2,1)S(1)}, bf16[3,384]{1,0:T(4,128)(2,1)S(1)}, u32[]{:S(2)}, u32[]{:S(2)}) collective-permute-start(bf16[3,384]{1,0:T(4,128)(2,1)S(1)} %slice.64), channel_id=1, source_target_pairs={{0,4},{4,8},{8,12},{12,16},{16,20},{20,24},{24,28},{1,5},{5,9},{9,... | collective-permute-start | bytes 6920 | tf_op jit(solution)/shard_map/ppermute | solution.py:10
  165.7 2.1 fusion
  167.8 21.4 %psum.28 = f32[4,384]{1,0:T(4,128)} all-reduce(f32[4,384]{1,0:T(4,128)S(1)} %pad_maximum_fusion), channel_id=1, replica_groups=mesh['ctx'=8,'ch'=4] {'ctx'}, use_global_device_ids=true, to_apply=%region_5.0 | all-reduce | flops 1536 | bytes 12288 | tf_op jit(solution)/shard_map/psum | solution.py:63
  189.2 27.3 %all-reduce.4.cloned.1.call-done = f32[1536,384]{0,1:T(8,128)} async-done(((f32[1536,384]{0,1:T(8,128)}), f32[1536,384]{0,1:T(8,128)}) %all-reduce.4.cloned.1.call-update) | async-done | bytes 2359312 | tf_op jit(solution)/shard_map/psum | solution.py:63
  216.5 3.0 copy.54
  219.5 3.0 convolution_bitcast_fusion.1
  222.5 1.9 copy.53
  224.4 54.3 %all-reduce.6.cloned.1.call-done = (f32[2,512,512]{2,1,0:T(8,128)}, f32[64,16,16]{2,1,0:T(8,128)}) async-done(((f32[2,512,512]{2,1,0:T(8,128)}, f32[64,16,16]{2,1,0:T(8,128)}), (f32[2,512,512]{2,1,0:T(8,128)}, f32[64,16,16]{2,1,0:T(8,128)})) %all-reduce.6.cloned.1.call-update) | async-done | bytes 2162704 | tf_op jit(solution)/shard_map/psum | solution.py:95
  278.7 1.9 copy.55
  280.6 38.5 %reduce-scatter.4.cloned.1.call-done = bf16[384,1024]{1,0:T(8,128)(2,1)} async-done(((bf16[1536,1024]{1,0:T(8,128)(2,1)}), bf16[384,1024]{1,0:T(8,128)(2,1)}) %reduce-scatter.4.cloned.1.call-update) | async-done | bytes 786448
  319.1 1.5 copy.59
  322.4 1.3 copy.76
  (53 shorter events, 20.0 us)
Async XLA Ops:
  7.2 60.4 %copy-start = (bf16[1536,384]{1,0:T(8,128)(2,1)S(1)}, bf16[1536,384]{1,0:T(8,128)(2,1)}, u32[]{:S(2)}) copy-start(bf16[1536,384]{1,0:T(8,128)(2,1)} %param.9) | copy-start | bytes 3538948
  7.2 60.4 %all-gather.2.cloned.1.call-start = ((), (), s32[]{:S(2)}) async-start(), calls=%async_computation.5 | async-start | bytes 3932160 | tf_op jit(solution)/shard_map/all_gather | solution.py:30
  10.1 9.0 %copy-start.6 = (bf16[64,16,16]{0,2,1:T(8,128)(2,1)S(1)}, bf16[64,16,16]{0,2,1:T(8,128)(2,1)}, u32[]{:S(2)}) copy-start(bf16[64,16,16]{0,2,1:T(8,128)(2,1)} %param.8) | copy-start | bytes 98308
  11.8 27.5 %all-to-all-start = ((bf16[2,512,384]{2,0,1:T(2,128)(2,1)}), bf16[2,512,384]{2,0,1:T(2,128)(2,1)S(1)}, u32[]{:S(2)}, u32[]{:S(2)}) async-start(bf16[2,512,384]{2,0,1:T(2,128)(2,1)} %copy.43), calls=%async_computation | async-start | bytes 1572864 | tf_op jit(solution)/shard_map/all_to_all | solution.py:23
  39.8 1.0 copy-start.3
  41.2 4.6 %copy-start.1 = (bf16[1024,384]{1,0:T(8,128)(2,1)S(1)}, bf16[1024,384]{1,0:T(8,128)(2,1)}, u32[]{:S(2)}) copy-start(bf16[1024,384]{1,0:T(8,128)(2,1)} %param.11) | copy-start | bytes 2359300
  42.3 24.0 %all-to-all-start.1 = ((bf16[16,64,384]{2,1,0:T(8,128)(2,1)}), bf16[16,64,384]{2,1,0:T(8,128)(2,1)S(1)}, u32[]{:S(2)}, u32[]{:S(2)}) async-start(bf16[16,64,384]{2,1,0:T(8,128)(2,1)} %copy.46), calls=%async_computation.1 | async-start | bytes 1572864 | tf_op jit(solution)/shard_map/all_to_all | solution.py:27
  45.8 6.2 %collective-permute-start.1 = (bf16[3,384]{1,0:T(4,128)(2,1)S(1)}, bf16[3,384]{1,0:T(4,128)(2,1)S(1)}, u32[]{:S(2)}, u32[]{:S(2)}) collective-permute-start(bf16[3,384]{1,0:T(4,128)(2,1)S(1)} %slice.59), channel_id=1, source_target_pairs={{4,0},{8,4},{12,8},{16,12},{20,16},{24,20},{28,24},{5,1},{9,5},{13... | collective-permute-start | bytes 6920 | tf_op jit(solution)/shard_map/ppermute | solution.py:10
  81.1 37.1 %all-to-all-start.2 = ((bf16[8,2,64,384]{3,2,1,0:T(8,128)(2,1)}), bf16[8,2,64,384]{3,2,1,0:T(8,128)(2,1)S(1)}, u32[]{:S(2)}, u32[]{:S(2)}) async-start(bf16[8,2,64,384]{3,2,1,0:T(8,128)(2,1)} %fusion.17), calls=%async_computation.2 | async-start | bytes 1572864 | tf_op jit(solution)/shard_map/all_to_all | solution.py:71
  85.1 131.4 %all-reduce.4.cloned.1.call-start = ((), (), s32[]{:S(2)}) async-start(), calls=%async_computation.6 | async-start | bytes 4718592 | tf_op jit(solution)/shard_map/psum | solution.py:63
  120.8 26.5 %all-to-all-start.3 = ((bf16[16,64,384]{2,1,0:T(8,128)(2,1)}), bf16[16,64,384]{2,1,0:T(8,128)(2,1)}, u32[]{:S(2)}, u32[]{:S(2)}) async-start(bf16[16,64,384]{2,1,0:T(8,128)(2,1)} %copy.50), calls=%async_computation.3 | async-start | bytes 1572864 | tf_op jit(solution)/shard_map/all_to_all | solution.py:87
  125.0 153.7 %all-reduce.6.cloned.1.call-start = ((), (), s32[]{:S(2)}) async-start(), calls=%async_computation.8 | async-start | bytes 5242880 | tf_op jit(solution)/shard_map/psum | solution.py:95
  126.5 22.0 %copy-start.2 = (bf16[1024,384]{1,0:T(8,128)(2,1)S(1)}, bf16[1024,384]{1,0:T(8,128)(2,1)}, u32[]{:S(2)}) copy-start(bf16[1024,384]{1,0:T(8,128)(2,1)} %param.6) | copy-start | bytes 2359300
  150.6 1.1 copy-start.7
  150.6 168.5 %reduce-scatter.4.cloned.1.call-start = ((), (), s32[]{:S(2)}) async-start(), calls=%async_computation.7 | async-start | bytes 3932160
  159.9 1.1 copy-start.5
  161.0 4.6 %collective-permute-start = (bf16[3,384]{1,0:T(4,128)(2,1)S(1)}, bf16[3,384]{1,0:T(4,128)(2,1)S(1)}, u32[]{:S(2)}, u32[]{:S(2)}) collective-permute-start(bf16[3,384]{1,0:T(4,128)(2,1)S(1)} %slice.64), channel_id=1, source_target_pairs={{0,4},{4,8},{8,12},{12,16},{16,20},{20,24},{24,28},{1,5},{5,9},{9,... | collective-permute-start | bytes 6920 | tf_op jit(solution)/shard_map/ppermute | solution.py:10
  320.6 1.9 copy-start.4
Sparse Core Ops, SparseCore 0:
  9.6 31.1 all-gather.1
  90.3 126.1 all-reduce.3
  219.6 59.0 all-reduce.5
  281.1 37.9 reduce-scatter.3
